TPU v7x, 32 devices: a whole 2x2x4 slice. The times are simulated.
32 devices in a mesh: seq: 4 (over z), shard: 8 (over y, x, core).
Axes of the slice: x: 2, y: 2, z: 4, core: 2. Of those that a mesh axis runs over, the one named last changes fastest.
Arguments:
- frames: bfloat16 [8, 1024, 1536], P('shard', 'seq'), may hold values from -6 to 6
- text_states: bfloat16 [8, 64, 1536], P('shard'), may hold values from -6 to 6
- norm_gain: bfloat16 [3, 1536], P(None, 'shard'), may hold values from 0.5 to 1.5
- norm_bias: bfloat16 [3, 1536], P(None, 'shard'), may hold values from -3 to 3
- self_project: bfloat16 [3, 1536, 1536], P(None, 'shard'), may hold values from -0.15625 to 0.15625
- self_output: bfloat16 [1536, 1536], P('shard'), may hold values from -1.75 to 1.75
- cross_project: bfloat16 [3, 1536, 1536], P(None, 'shard'), may hold values from -0.15625 to 0.15625
- cross_output: bfloat16 [1536, 1536], P('shard'), may hold values from -0.625 to 0.625
- up_weight: bfloat16 [1536, 6144], P('shard'), may hold values from -0.15625 to 0.15625
- down_weight: bfloat16 [6144, 1536], P('shard'), may hold values from -0.078125 to 0.078125
- cotangent: bfloat16 [8, 1024, 1536], P('shard', 'seq'), may hold values from -6 to 6
Outputs:
- output: bfloat16 [8, 1024, 1536], P('shard', 'seq')
- frames_grad: float32 [8, 1024, 1536], P('shard', 'seq')
- text_grad: float32 [8, 64, 1536], P('shard')
- gain_grad: float32 [3, 1536], P(None, 'shard')
- bias_grad: float32 [3, 1536], P(None, 'shard')
- self_project_grad: float32 [3, 1536, 1536], P(None, 'shard')
- self_output_grad: float32 [1536, 1536], P('shard')
- cross_project_grad: float32 [3, 1536, 1536], P(None, 'shard')
- cross_output_grad: float32 [1536, 1536], P('shard')
- up_grad: float32 [1536, 6144], P('shard')
- down_grad: float32 [6144, 1536], P('shard')
All inputs are finite; a program needn't handle non-finite values.
Results may differ from a plain program's by a relative error of at most 0.022.
Values may be sent and summed in bfloat16 or wider, within the bound.
No kernel may reach another device: no remote copies, remote signals or barrier semaphores. Data moves between devices by JAX's collectives and lax.ppermute only.
A program may use at most 384 MiB of HBM per device.

v0:
```python
import jax
import jax.numpy as jnp
from jax import lax
from jax.sharding import PartitionSpec as P

HEAD_DIM = 64
QBLOCK = 512
EPSILON = 1e-05
MASKED_SCORE = -1e30


def layer_norm(hidden, gain, shift):
    center = hidden - jnp.mean(hidden, axis=-1, keepdims=True)
    spread = lax.rsqrt(jnp.mean(center * center, axis=-1, keepdims=True) + EPSILON)
    return center * spread * gain + shift


def exact_gelu(values):
    return jax.nn.gelu(values, approximate=False)


def contract(form, left, right):
    return jnp.einsum(form, left, right, preferred_element_type=jnp.float32)


def split_heads(values):
    return values.reshape(values.shape[:-1] + (values.shape[-1] // HEAD_DIM, HEAD_DIM))


def join_heads(values):
    return values.reshape(values.shape[:-2] + (values.shape[-2] * values.shape[-1],))


def causal_visible(start_row, row_count, stop_row):
    row_place = start_row + lax.broadcasted_iota(jnp.int32, (row_count, stop_row), 0)
    column_place = lax.broadcasted_iota(jnp.int32, (row_count, stop_row), 1)
    return column_place <= row_place


def block_scores(queries, key_rows, start_row, stop_row, scaling):
    scores = (
        contract("cqhe,ckhe->chqk", queries[:, start_row:stop_row], key_rows[:, :stop_row])
        * scaling
    )
    return jnp.where(
        causal_visible(start_row, stop_row - start_row, stop_row), scores, MASKED_SCORE
    )


def self_forward(queries, key_rows, value_rows, scaling):
    length = queries.shape[1]
    outputs = []
    totals = []
    for start_row in range(0, length, QBLOCK):
        stop_row = start_row + QBLOCK
        scores = block_scores(queries, key_rows, start_row, stop_row, scaling)
        largest = jnp.max(scores, axis=-1, keepdims=True)
        weights = jnp.exp(scores - largest)
        summed = jnp.sum(weights, axis=-1, keepdims=True)
        shares = (weights / summed).astype(jnp.bfloat16)
        outputs.append(contract("chqk,ckhe->cqhe", shares, value_rows[:, :stop_row]))
        totals.append(largest + jnp.log(summed))
    return (jnp.concatenate(outputs, axis=1), totals)


def self_backward(queries, key_rows, value_rows, totals, grad_out, scaling):
    length = queries.shape[1]
    grad_queries = []
    grad_keys = jnp.zeros(key_rows.shape, jnp.float32)
    grad_values = jnp.zeros(value_rows.shape, jnp.float32)
    for number, start_row in enumerate(range(0, length, QBLOCK)):
        stop_row = start_row + QBLOCK
        query_block = queries[:, start_row:stop_row]
        grad_block = grad_out[:, start_row:stop_row]
        scores = block_scores(queries, key_rows, start_row, stop_row, scaling)
        shares = jnp.exp(scores - totals[number])
        grad_shares = contract("cqhe,ckhe->chqk", grad_block, value_rows[:, :stop_row])
        centred = jnp.sum(shares * grad_shares, axis=-1, keepdims=True)
        grad_scores = (shares * (grad_shares - centred)).astype(jnp.bfloat16)
        grad_queries.append(
            contract("chqk,ckhe->cqhe", grad_scores, key_rows[:, :stop_row]) * scaling
        )
        grad_keys = grad_keys.at[:, :stop_row].add(
            contract("chqk,cqhe->ckhe", grad_scores, query_block) * scaling
        )
        grad_values = grad_values.at[:, :stop_row].add(
            contract("chqk,cqhe->ckhe", shares.astype(jnp.bfloat16), grad_block)
        )
    return (jnp.concatenate(grad_queries, axis=1), grad_keys, grad_values)


def cross_softmax(queries, key_rows, scaling):
    scores = contract("cfhe,cxhe->chxf", queries, key_rows) * scaling
    largest = jnp.max(scores, axis=2, keepdims=True)
    weights = jnp.exp(scores - largest)
    return weights / jnp.sum(weights, axis=2, keepdims=True)


def fetch_self(self_project, self_output, norm_gain, norm_bias):
    return (
        lax.all_gather(self_project, "shard", axis=1, tiled=True),
        lax.all_gather(self_output, "shard", axis=0, tiled=True),
        lax.all_gather(norm_gain, "shard", axis=1, tiled=True),
        lax.all_gather(norm_bias, "shard", axis=1, tiled=True),
    )


def fetch_cross(cross_project, cross_output):
    return (
        lax.all_gather(cross_project, "shard", axis=1, tiled=True),
        lax.all_gather(cross_output, "shard", axis=0, tiled=True),
    )


def fetch_mlp(up_weight, down_weight):
    return (
        lax.all_gather(up_weight, "shard", axis=0, tiled=True),
        lax.all_gather(down_weight, "shard", axis=0, tiled=True),
    )


def body(
    frames,
    text_states,
    norm_gain,
    norm_bias,
    self_project,
    self_output,
    cross_project,
    cross_output,
    up_weight,
    down_weight,
    cotangent,
):
    scaling = HEAD_DIM ** (-0.5)
    project_all, output_all, gain_all, bias_all = fetch_self(
        self_project, self_output, norm_gain, norm_bias
    )
    gains = gain_all.astype(jnp.float32)
    biases = bias_all.astype(jnp.float32)
    hidden = frames.astype(jnp.float32)
    normed_one, norm_pull_one = jax.vjp(layer_norm, hidden, gains[0], biases[0])
    inputs_one = normed_one.astype(jnp.bfloat16)
    projected = contract("cfd,jde->jcfe", inputs_one, project_all).astype(jnp.bfloat16)
    by_heads = lax.all_to_all(projected, "seq", split_axis=3, concat_axis=2, tiled=True)
    queries = split_heads(by_heads[0])
    key_rows = split_heads(by_heads[1])
    value_rows = split_heads(by_heads[2])
    attended_heads, totals = self_forward(queries, key_rows, value_rows, scaling)
    attended = lax.all_to_all(
        join_heads(attended_heads).astype(jnp.bfloat16),
        "seq",
        split_axis=1,
        concat_axis=2,
        tiled=True,
    )
    hidden_one = hidden + contract("cfd,de->cfe", attended, output_all)
    cross_all, cross_out_all = fetch_cross(cross_project, cross_output)
    normed_two, norm_pull_two = jax.vjp(layer_norm, hidden_one, gains[1], biases[1])
    inputs_two = normed_two.astype(jnp.bfloat16)
    cross_queries = contract("cfd,de->cfe", inputs_two, cross_all[0]).astype(jnp.bfloat16)
    cross_pairs = contract("cxd,jde->jcxe", text_states, cross_all[1:]).astype(jnp.bfloat16)
    text_keys = split_heads(cross_pairs[0])
    text_values = split_heads(cross_pairs[1])
    cross_shares = cross_softmax(split_heads(cross_queries), text_keys, scaling)
    cross_low = cross_shares.astype(jnp.bfloat16)
    mixed_text = join_heads(contract("chxf,cxhe->cfhe", cross_low, text_values)).astype(
        jnp.bfloat16
    )
    hidden_two = hidden_one + contract("cfd,de->cfe", mixed_text, cross_out_all)
    up_all, down_all = fetch_mlp(up_weight, down_weight)
    normed_three, norm_pull_three = jax.vjp(layer_norm, hidden_two, gains[2], biases[2])
    inputs_three = normed_three.astype(jnp.bfloat16)
    before_act = contract("cfd,dk->cfk", inputs_three, up_all)
    activated, gelu_pull = jax.vjp(exact_gelu, before_act)
    activated_low = activated.astype(jnp.bfloat16)
    result = hidden_two + contract("cfk,kd->cfd", activated_low, down_all)
    output = result.astype(jnp.bfloat16)
    up_all, down_all = fetch_mlp(up_weight, down_weight)
    grad_result = cotangent.astype(jnp.float32)
    grad_down = contract("cfk,cfd->kd", activated_low, cotangent)
    grad_act = contract("cfd,kd->cfk", cotangent, down_all)
    grad_before = gelu_pull(grad_act)[0].astype(jnp.bfloat16)
    grad_up = contract("cfd,cfk->dk", inputs_three, grad_before)
    grad_inputs_three = contract("cfk,dk->cfd", grad_before, up_all)
    grad_two_part, gain_three, bias_three = norm_pull_three(grad_inputs_three)
    grad_hidden_two = grad_result + grad_two_part
    up_share, down_share = (
        lax.psum_scatter(
            grad_up.astype(jnp.bfloat16), "shard", scatter_dimension=0, tiled=True
        ).astype(jnp.float32),
        lax.psum_scatter(
            grad_down.astype(jnp.bfloat16), "shard", scatter_dimension=0, tiled=True
        ).astype(jnp.float32),
    )
    cross_all, cross_out_all = fetch_cross(cross_project, cross_output)
    grad_low_two = grad_hidden_two.astype(jnp.bfloat16)
    grad_cross_out = contract("cfd,cfe->de", mixed_text, grad_low_two)
    grad_mixed = split_heads(
        contract("cfe,de->cfd", grad_low_two, cross_out_all).astype(jnp.bfloat16)
    )
    grad_shares = contract("cfhe,cxhe->chxf", grad_mixed, text_values)
    centred = jnp.sum(cross_shares * grad_shares, axis=2, keepdims=True)
    grad_scores = (cross_shares * (grad_shares - centred)).astype(jnp.bfloat16)
    grad_cross_query = join_heads(
        contract("chxf,cxhe->cfhe", grad_scores, text_keys) * scaling
    ).astype(jnp.bfloat16)
    grad_text_keys = join_heads(
        contract("chxf,cfhe->cxhe", grad_scores, split_heads(cross_queries)) * scaling
    )
    grad_text_values = join_heads(contract("chxf,cfhe->cxhe", cross_low, grad_mixed))
    grad_pairs = lax.psum(jnp.stack([grad_text_keys, grad_text_values]).astype(jnp.bfloat16), "seq")
    grad_text = contract("jcxe,jde->cxd", grad_pairs, cross_all[1:])
    grad_cross_pairs = contract("cxd,jcxe->jde", text_states, grad_pairs)
    grad_cross_first = contract("cfd,cfe->de", inputs_two, grad_cross_query)
    grad_inputs_two = contract("cfe,de->cfd", grad_cross_query, cross_all[0])
    grad_one_part, gain_two, bias_two = norm_pull_two(grad_inputs_two)
    grad_hidden_one = grad_hidden_two + grad_one_part
    cross_stack = jnp.concatenate([grad_cross_first[None], grad_cross_pairs], axis=0)
    cross_share, cross_out_share = (
        lax.psum_scatter(
            cross_stack.astype(jnp.bfloat16), "shard", scatter_dimension=1, tiled=True
        ).astype(jnp.float32),
        lax.psum_scatter(
            grad_cross_out.astype(jnp.bfloat16), "shard", scatter_dimension=0, tiled=True
        ).astype(jnp.float32),
    )
    project_all, output_all, gain_all, bias_all = fetch_self(
        self_project, self_output, norm_gain, norm_bias
    )
    grad_low_one = grad_hidden_one.astype(jnp.bfloat16)
    grad_self_out = contract("cfd,cfe->de", attended, grad_low_one)
    grad_attended = contract("cfe,de->cfd", grad_low_one, output_all).astype(jnp.bfloat16)
    grad_heads = lax.all_to_all(grad_attended, "seq", split_axis=2, concat_axis=1, tiled=True)
    grad_queries, grad_keys, grad_values = self_backward(
        queries, key_rows, value_rows, totals, split_heads(grad_heads), scaling
    )
    grad_stacked = jnp.stack(
        [join_heads(grad_queries), join_heads(grad_keys), join_heads(grad_values)]
    ).astype(jnp.bfloat16)
    grad_projected = lax.all_to_all(grad_stacked, "seq", split_axis=2, concat_axis=3, tiled=True)
    grad_self_project = contract("cfd,jcfe->jde", inputs_one, grad_projected)
    grad_inputs_one = contract("jcfe,jde->cfd", grad_projected, project_all)
    grad_zero_part, gain_one, bias_one = norm_pull_one(grad_inputs_one)
    grad_frames = grad_hidden_one + grad_zero_part
    gain_stack = jnp.stack([gain_one, gain_two, gain_three])
    bias_stack = jnp.stack([bias_one, bias_two, bias_three])
    project_share, output_share, gain_share, bias_share = (
        lax.psum_scatter(
            grad_self_project.astype(jnp.bfloat16), "shard", scatter_dimension=1, tiled=True
        ).astype(jnp.float32),
        lax.psum_scatter(
            grad_self_out.astype(jnp.bfloat16), "shard", scatter_dimension=0, tiled=True
        ).astype(jnp.float32),
        lax.psum_scatter(
            gain_stack.astype(jnp.bfloat16), "shard", scatter_dimension=1, tiled=True
        ).astype(jnp.float32),
        lax.psum_scatter(
            bias_stack.astype(jnp.bfloat16), "shard", scatter_dimension=1, tiled=True
        ).astype(jnp.float32),
    )
    summed_parts = (
        lax.psum(project_share.astype(jnp.bfloat16), "seq").astype(jnp.float32),
        lax.psum(output_share.astype(jnp.bfloat16), "seq").astype(jnp.float32),
        lax.psum(cross_share[:1].astype(jnp.bfloat16), "seq").astype(jnp.float32),
        lax.psum(cross_out_share.astype(jnp.bfloat16), "seq").astype(jnp.float32),
        lax.psum(up_share.astype(jnp.bfloat16), "seq").astype(jnp.float32),
        lax.psum(down_share.astype(jnp.bfloat16), "seq").astype(jnp.float32),
        lax.psum(gain_share.astype(jnp.bfloat16), "seq").astype(jnp.float32),
        lax.psum(bias_share.astype(jnp.bfloat16), "seq").astype(jnp.float32),
    )
    cross_final = jnp.concatenate([summed_parts[2], cross_share[1:]], axis=0)
    return (
        output,
        grad_frames,
        grad_text,
        summed_parts[6],
        summed_parts[7],
        summed_parts[0],
        summed_parts[1],
        cross_final,
        summed_parts[3],
        summed_parts[4],
        summed_parts[5],
    )


def solution(mesh):
    return jax.shard_map(
        body,
        mesh=mesh,
        in_specs=(
            P("shard", "seq", None),
            P("shard", None, None),
            P(None, "shard"),
            P(None, "shard"),
            P(None, "shard", None),
            P("shard", None),
            P(None, "shard", None),
            P("shard", None),
            P("shard", None),
            P("shard", None),
            P("shard", "seq", None),
        ),
        out_specs=(
            P("shard", "seq", None),
            P("shard", "seq", None),
            P("shard", None, None),
            P(None, "shard"),
            P(None, "shard"),
            P(None, "shard", None),
            P("shard", None),
            P(None, "shard", None),
            P("shard", None),
            P("shard", None),
            P("shard", None),
        ),
        check_vma=False,
    )
```

profile of v0, /device:TPU:0, one launch (start us, length us, event | category | flops | bytes accessed | tf_op | source)
XLA Modules:
  0.0 1739.3 jit_solution(10451731953631284153)
XLA Ops:
  31.7 59.6 %all-gather.9.cloned.1.call-done = bf16[3,1536,1536]{2,1,0:T(8,128)(2,1)} async-done(((bf16[3,192,1536]{2,1,0:T(8,128)(2,1)}), bf16[3,1536,1536]{2,1,0:T(8,128)(2,1)}) %all-gather.9.cloned.1.call-update) | async-done | bytes 14155792 | tf_op jit(solution)/shard_map/all_gather | solution.py:101
  111.2 69.5 %all-to-all-done = bf16[3,1,256,1536]{2,0,1,3:T(4,128)(2,1)} async-done(((bf16[3,1,256,1536]{2,0,1,3:T(4,128)(2,1)}), bf16[3,1,256,1536]{2,0,1,3:T(4,128)(2,1)}, u32[]{:S(2)}, u32[]{:S(2)}) %all-to-all-start) | async-done | bytes 2359328 | tf_op jit(solution)/shard_map/all_to_all | solution.py:145
  228.0 11.9 all-to-all-done.1
  261.1 92.5 %all-gather.17.cloned.1.call-done = bf16[1536,6144]{1,0:T(8,128)(2,1)} async-done(((bf16[192,6144]{1,0:T(8,128)(2,1)}), bf16[1536,6144]{1,0:T(8,128)(2,1)}) %all-gather.17.cloned.1.call-update) | async-done | bytes 18874384 | tf_op jit(solution)/shard_map/all_gather | solution.py:117
  353.6 23.7 %multiply_convert_fusion.2 = (bf16[256,6144]{1,0:T(8,128)(2,1)}, f32[256,6144]{1,0:T(8,128)}, f32[256,6144]{1,0:T(8,128)}) fusion(bf16[1536,6144]{1,0:T(8,128)(2,1)} %all-gather.17.cloned.1.call-done, f32[1,256,1536]{2,1,0:T(8,128)S(1)} %get-tuple-element.192, f32[1536]{0:T(1024)S(1)} %get-tuple-element.161, f32[1536]{0:T(1024)S(1)} %get-tuple-element.206, ...), kind=kOutput, calls=%fused_computation.31 | convolution fusion | flops 4936040448 | bytes 36190208 | tf_op jit(solution)/shard_map/cfd,dk->cfk/dot_general | solution.py:23
  377.3 76.7 %all-gather.19.cloned.1.call-done = bf16[6144,1536]{1,0:T(8,128)(2,1)} async-done(((bf16[768,1536]{1,0:T(8,128)(2,1)}), bf16[6144,1536]{1,0:T(8,128)(2,1)}) %all-gather.19.cloned.1.call-update) | async-done | bytes 18874384 | tf_op jit(solution)/shard_map/all_gather | solution.py:118
  453.9 14.8 add_convert_fusion
  513.5 24.0 %all-reduce.7.cloned.1.call-done = bf16[2,64,1536]{2,1,0:T(8,128)(2,1)} async-done(((bf16[2,64,1536]{2,1,0:T(8,128)(2,1)}), bf16[2,64,1536]{2,1,0:T(8,128)(2,1)}) %all-reduce.7.cloned.1.call-update) | async-done | bytes 393232 | tf_op jit(solution)/shard_map/psum | solution.py:212
  547.7 30.8 %copy.225 = bf16[3,1536,1536]{2,0,1:T(4,128)(2,1)} copy(bf16[3,1536,1536]{1,2,0:T(8,128)(2,1)} %pad_maximum_fusion) | data formatting | bytes 28311552
  578.5 17.0 copy.233
  620.5 18.2 %all-to-all-done.2 = bf16[4,2,49152]{2,1,0:T(2,128)(2,1)S(1)} async-done(((bf16[4,2,49152]{2,1,0:T(2,128)(2,1)}), bf16[4,2,49152]{2,1,0:T(2,128)(2,1)S(1)}, u32[]{:S(2)}, u32[]{:S(2)}) %all-to-all-start.2) | async-done | bytes 786464 | tf_op jit(solution)/shard_map/all_to_all | solution.py:234
  709.7 72.8 %all_to_all.60 = bf16[3,1,1024,384]{3,0,1,2:T(4,128)(2,1)S(1)} all-to-all(bf16[3,1,1024,384]{3,0,1,2:T(4,128)(2,1)S(1)} %pad_maximum_fusion.1), channel_id=1, replica_groups=mesh['seq'=4,'shard'=8] {'seq'}, dimensions={2} | all-to-all | bytes 4718592 | tf_op jit(solution)/shard_map/all_to_all | solution.py:241
  797.7 30.8 %copy.223 = bf16[3,1536,1536]{2,0,1:T(4,128)(2,1)} copy(bf16[3,1536,1536]{1,2,0:T(8,128)(2,1)} %convert_bitcast_fusion) | data formatting | bytes 28311552
  828.6 17.0 copy.232
  858.2 12.6 convolution_convert_fusion.1
  906.5 40.3 %reduce-scatter.29.cloned.1.call-done = bf16[192,4608]{1,0:T(8,128)(2,1)} async-done(((bf16[1536,4608]{1,0:T(8,128)(2,1)}), bf16[192,4608]{1,0:T(8,128)(2,1)}) %reduce-scatter.29.cloned.1.call-update) | async-done | bytes 1769488
  957.5 46.9 %reduce-scatter.19.cloned.1.call-done = bf16[192,1536]{1,0:T(8,128)(2,1)} async-done(((bf16[1536,1536]{1,0:T(8,128)(2,1)}), bf16[192,1536]{1,0:T(8,128)(2,1)}) %reduce-scatter.19.cloned.1.call-update) | async-done | bytes 589840 | tf_op jit(solution)/shard_map/reduce_scatter | solution.py:224
  1004.5 57.8 %reduce-scatter.17.cloned.1.call-done = bf16[192,1536]{1,0:T(8,128)(2,1)} async-done(((bf16[1536,1536]{1,0:T(8,128)(2,1)}), bf16[192,1536]{1,0:T(8,128)(2,1)}) %reduce-scatter.17.cloned.1.call-update) | async-done | bytes 589840 | tf_op jit(solution)/shard_map/reduce_scatter | solution.py:252
  1062.3 129.9 %reduce-scatter.21.cloned.1.call-done = bf16[192,6144]{1,0:T(8,128)(2,1)} async-done(((bf16[1536,6144]{1,0:T(8,128)(2,1)}), bf16[192,6144]{1,0:T(8,128)(2,1)}) %reduce-scatter.21.cloned.1.call-update) | async-done | bytes 2359312 | tf_op jit(solution)/shard_map/reduce_scatter | solution.py:189
  1192.2 130.1 %reduce-scatter.23.cloned.1.call-done = bf16[768,1536]{1,0:T(8,128)(2,1)} async-done(((bf16[6144,1536]{1,0:T(8,128)(2,1)}), bf16[768,1536]{1,0:T(8,128)(2,1)}) %reduce-scatter.23.cloned.1.call-update) | async-done | bytes 2359312 | tf_op jit(solution)/shard_map/reduce_scatter | solution.py:192
  1343.7 15.4 reduce-scatter.25.cloned.1.call-done
  1360.0 35.9 %reduce-scatter.27.cloned.1.call-done = bf16[192,3]{1,0:T(8,128)(2,1)} async-done(((bf16[1536,3]{1,0:T(8,128)(2,1)}), bf16[192,3]{1,0:T(8,128)(2,1)}) %reduce-scatter.27.cloned.1.call-update) | async-done | bytes 1168
  1396.8 11.9 all-reduce.2
  1414.7 297.1 %all-reduce.9.cloned.1.call-done = (bf16[3,192,1536]{1,2,0:T(8,128)(2,1)}, bf16[192,1536]{1,0:T(8,128)(2,1)}, bf16[1,192,1536]{1,2,0:T(8,128)(2,1)}, bf16[192,15...) async-done(((bf16[3,192,1536]{1,2,0:T(8,128)(2,1)}, bf16[192,1536]{1,0:T(8,128)(2,1)}, bf16[1,192,1536]{1,2,0:T(8,128)(2,1)}, ...) | async-done | bytes 8257552 | tf_op jit(solution)/shard_map/psum | solution.py:263
  (380 shorter events, 386.4 us)
Async XLA Ops:
  7.2 84.2 %all-gather.9.cloned.1.call-start = ((), (), s32[]{:S(2)}) async-start(), calls=%async_computation.12 | async-start | bytes 15925248 | tf_op jit(solution)/shard_map/all_gather | solution.py:101
  7.9 212.1 %all-gather.13.cloned.1.call-start = ((), (), s32[]{:S(2)}) async-start(), calls=%async_computation.14 | async-start | bytes 15925248 | tf_op jit(solution)/shard_map/all_gather | solution.py:110
  8.7 232.6 %all-gather.11.cloned.1.call-start = ((), (), s32[]{:S(2)}) async-start(), calls=%async_computation.13 | async-start | bytes 5308416 | tf_op jit(solution)/shard_map/all_gather | solution.py:102
  9.4 247.2 %all-gather.15.cloned.1.call-start = ((), (), s32[]{:S(2)}) async-start(), calls=%async_computation.15 | async-start | bytes 5308416 | tf_op jit(solution)/shard_map/all_gather | solution.py:111
  10.0 343.6 %all-gather.17.cloned.1.call-start = ((), (), s32[]{:S(2)}) async-start(), calls=%async_computation.16 | async-start | bytes 21233664 | tf_op jit(solution)/shard_map/all_gather | solution.py:117
  10.6 443.3 %all-gather.19.cloned.1.call-start = ((), (), s32[]{:S(2)}) async-start(), calls=%async_computation.17 | async-start | bytes 21233664 | tf_op jit(solution)/shard_map/all_gather | solution.py:118
  31.1 214.7 %copy-start.67 = (f32[1536]{0:T(1024)}, f32[1536]{0:T(1024)S(1)}, u32[]{:S(2)}) copy-start(f32[1536]{0:T(1024)S(1)} %get-tuple-element.205) | copy-start | bytes 18436
  31.1 214.7 %copy-start.83 = (f32[1536]{0:T(1024)}, f32[1536]{0:T(1024)S(1)}, u32[]{:S(2)}) copy-start(f32[1536]{0:T(1024)S(1)} %get-tuple-element.162) | copy-start | bytes 18436
  31.1 322.4 %copy-start.56 = (f32[1536]{0:T(1024)}, f32[1536]{0:T(1024)S(1)}, u32[]{:S(2)}) copy-start(f32[1536]{0:T(1024)S(1)} %get-tuple-element.161) | copy-start | bytes 18436
  104.3 76.4 %all-to-all-start = ((bf16[3,1,256,1536]{2,0,1,3:T(4,128)(2,1)}), bf16[3,1,256,1536]{2,0,1,3:T(4,128)(2,1)}, u32[]{:S(2)}, u32[]{:S(2)}) async-start(bf16[3,1,256,1536]{2,0,1,3:T(4,128)(2,1)} %copy.187), calls=%async_computation | async-start | bytes 6291456 | tf_op jit(solution)/shard_map/all_to_all | solution.py:145
  216.4 23.5 %all-to-all-start.1 = ((bf16[4,2,49152]{2,1,0:T(2,128)(2,1)}), bf16[4,2,49152]{2,1,0:T(2,128)(2,1)S(1)}, u32[]{:S(2)}, u32[]{:S(2)}) async-start(bf16[4,2,49152]{2,1,0:T(2,128)(2,1)} %reshape.954), calls=%async_computation.1 | async-start | bytes 1572864 | tf_op jit(solution)/shard_map/all_to_all | solution.py:150
  220.0 317.6 %all-reduce.7.cloned.1.call-start = ((), (), s32[]{:S(2)}) async-start(), calls=%async_computation.18 | async-start | bytes 786432 | tf_op jit(solution)/shard_map/psum | solution.py:212
  254.0 237.8 %copy-start.58 = (f32[24,256]{1,0:T(8,128)}, f32[24,256]{1,0:T(8,128)S(1)}, u32[]{:S(2)}) copy-start(f32[24,256]{1,0:T(8,128)S(1)} %get-tuple-element.189) | copy-start | bytes 73732
  260.8 218.7 %copy-start.9 = (f32[1,256,1536]{2,1,0:T(8,128)}, f32[1,256,1536]{2,1,0:T(8,128)S(1)}, u32[]{:S(2)}) copy-start(f32[1,256,1536]{2,1,0:T(8,128)S(1)} %get-tuple-element.192) | copy-start | bytes 4718596
  500.4 396.8 %reduce-scatter.31.cloned.1.call-start = ((), (), s32[]{:S(2)}) async-start(), calls=%async_computation.26 | async-start | bytes 15925248
  616.7 22.0 %all-to-all-start.2 = ((bf16[4,2,49152]{2,1,0:T(2,128)(2,1)}), bf16[4,2,49152]{2,1,0:T(2,128)(2,1)S(1)}, u32[]{:S(2)}, u32[]{:S(2)}) async-start(bf16[4,2,49152]{2,1,0:T(2,128)(2,1)} %reshape.956), calls=%async_computation.2 | async-start | bytes 1572864 | tf_op jit(solution)/shard_map/all_to_all | solution.py:234
  620.5 326.3 %reduce-scatter.29.cloned.1.call-start = ((), (), s32[]{:S(2)}) async-start(), calls=%async_computation.25 | async-start | bytes 15925248
  845.6 158.8 %reduce-scatter.19.cloned.1.call-start = ((), (), s32[]{:S(2)}) async-start(), calls=%async_computation.20 | async-start | bytes 5308416 | tf_op jit(solution)/shard_map/reduce_scatter | solution.py:224
  851.5 210.8 %reduce-scatter.17.cloned.1.call-start = ((), (), s32[]{:S(2)}) async-start(), calls=%async_computation.19 | async-start | bytes 5308416 | tf_op jit(solution)/shard_map/reduce_scatter | solution.py:252
  857.6 334.7 %reduce-scatter.21.cloned.1.call-start = ((), (), s32[]{:S(2)}) async-start(), calls=%async_computation.21 | async-start | bytes 21233664 | tf_op jit(solution)/shard_map/reduce_scatter | solution.py:189
  870.8 451.5 %reduce-scatter.23.cloned.1.call-start = ((), (), s32[]{:S(2)}) async-start(), calls=%async_computation.22 | async-start | bytes 21233664 | tf_op jit(solution)/shard_map/reduce_scatter | solution.py:192
  882.3 476.8 %reduce-scatter.25.cloned.1.call-start = ((), (), s32[]{:S(2)}) async-start(), calls=%async_computation.23 | async-start | bytes 442368
  895.9 500.1 %reduce-scatter.27.cloned.1.call-start = ((), (), s32[]{:S(2)}) async-start(), calls=%async_computation.24 | async-start | bytes 442368
  897.0 814.8 %all-reduce.9.cloned.1.call-start = ((), (), s32[]{:S(2)}) async-start(), calls=%async_computation.27 | async-start | bytes 18087936 | tf_op jit(solution)/shard_map/psum | solution.py:263
  (91 other events, 1119.1 us)
Sparse Core Ops, SparseCore 0:
  9.9 81.4 all-gather.8
  93.3 78.6 all-gather.12
  173.8 38.7 all-gather.10
  214.4 38.7 all-gather.14
  255.0 98.5 all-gather.16
  355.3 98.5 all-gather.18
  500.6 36.9 all-reduce.6
  595.7 101.5 reduce-scatter.30
  845.8 100.9 reduce-scatter.28
  950.6 53.7 reduce-scatter.18
  1008.5 53.7 reduce-scatter.16
  1065.8 126.4 reduce-scatter.20
  1195.8 126.4 reduce-scatter.22
  1325.2 33.8 reduce-scatter.24
  1362.0 33.8 reduce-scatter.26
  1399.6 312.1 all-reduce.8
where the time goes:
time: 1750 us; the launch traced here: 1740 us
  waiting for transfers between devices  1110 us (63%)
  matrix products  220 us (13%)
  local copies, waits for them, and re-layouts  207 us (12%)
  blocking collectives  104 us (6%)
  other arithmetic  70.1 us (4%)
    psum x1, waiting for transfers between devices, body(): lax.psum(project_share.astype(jnp.bfloat16), 'seq').astype(jnp.float32)  297 us
    dot_general x38, matrix products, contract(): return jnp.einsum(form, left, right, preferred_element_type=jnp.float32)  218 us
    unnamed x214, local copies, waits for them, and re-layouts  146 us
    reduce_scatter x1, waiting for transfers between devices, body(): lax.psum_scatter(grad_down.astype(jnp.bfloat16), 'shard', scatter_dimensi...  130 us
    reduce_scatter x1, waiting for transfers between devices, body(): lax.psum_scatter(grad_up.astype(jnp.bfloat16), 'shard', scatter_dimension...  130 us
    unnamed x20, waiting for transfers between devices  95.5 us
    all_gather x1, waiting for transfers between devices, fetch_mlp(): lax.all_gather(up_weight, 'shard', axis=0, tiled=True)  92.5 us
    all_gather x1, waiting for transfers between devices, fetch_mlp(): lax.all_gather(down_weight, 'shard', axis=0, tiled=True)  76.7 us
  transfers between devices with their start and end apart: 19, of which 15 were waited for; matrix products, arithmetic and copies ran while one was open for 21% of the time, Pallas kernels for 0%

commit v1 on v0

--- a/solution.py
+++ b/solution.py
@@ -7,6 +7,28 @@
 QBLOCK = 512
 EPSILON = 1e-05
 MASKED_SCORE = -1e30
+
+
+def joined_along(blocks, dim):
+    shape = list(blocks.shape[1:])
+    shape[dim] *= blocks.shape[0]
+    return jnp.moveaxis(blocks, 0, dim).reshape(shape)
+
+
+def grow_blocks(x, axis):
+    size = lax.axis_size(axis)
+    blocks = x[None]
+    for level in range(size.bit_length() - 1):
+        bit = 1 << level
+        other = lax.ppermute(blocks, axis, [(i, i ^ bit) for i in range(size)])
+        both = jnp.stack([blocks, other])
+        upper = lax.axis_index(axis) >> level & 1
+        blocks = jnp.where(upper == 0, both, both[::-1]).reshape(-1, *x.shape)
+    return blocks
+
+
+def collect(x, axis, dim):
+    return joined_along(grow_blocks(x, axis), dim)
 
 
 def layer_norm(hidden, gain, shift):
@@ -115,7 +137,7 @@
 def fetch_mlp(up_weight, down_weight):
     return (
         lax.all_gather(up_weight, "shard", axis=0, tiled=True),
-        lax.all_gather(down_weight, "shard", axis=0, tiled=True),
+        collect(down_weight, "shard", 0),
     )
 
 

time: 1750 us -> 2080 us (1.19)
  blocking collectives: 104 us -> 428 us
  waiting for transfers between devices: 1110 us -> 1030 us
  other arithmetic: 70.1 us -> 140 us
    all_gather x1, blocking collectives: 10.4 us -> 335 us  [fetch_self(): lax.all_gather(norm_gain, 'shard', axis=1, tiled=True)]
    ppermute x0 -> x3, waiting for transfers between devices: none -> 180 us  [grow_blocks(): other = lax.ppermute(blocks, axis, [(i, i ^ bit) for i in range(size)])]
    all_gather x1, waiting for transfers between devices: 92.5 us -> 0.02 us  [fetch_mlp(): lax.all_gather(up_weight, 'shard', axis=0, tiled=True)]
    all_gather x1 -> x0, waiting for transfers between devices: 76.7 us -> none  [fetch_mlp(): lax.all_gather(down_weight, 'shard', axis=0, tiled=True)]
    all_gather x1, waiting for transfers between devices: 59.6 us -> 0.02 us  [fetch_self(): lax.all_gather(self_project, 'shard', axis=1, tiled=True)]
    select_n x0 -> x2, other arithmetic: none -> 36.1 us  [grow_blocks(): blocks = jnp.where(upper == 0, both, both[::-1]).reshape(-1, *x.shape)]
    another operation x2 -> x6, other arithmetic: 1.03 us -> 34.8 us  [the longest x4 33.7 us: grow_blocks(): both = jnp.stack([blocks, other])]
    unnamed x20 -> x19, waiting for transfers between devices: 95.5 us -> 95.2 us
  transfers between devices with their start and end apart: 19 -> 21, of which waited for: 15 -> 13; matrix products, arithmetic and copies ran while one was open for 21% -> 20% of each run, Pallas kernels for 0% -> 0%
where the time goes in v1:
time: 2080 us; the launch traced here: 2070 us
  waiting for transfers between devices  1030 us (50%)
  blocking collectives  428 us (21%)
  matrix products  226 us (11%)
  local copies, waits for them, and re-layouts  207 us (10%)
  other arithmetic  140 us (7%)
    all_gather x1, blocking collectives, fetch_self(): lax.all_gather(norm_gain, 'shard', axis=1, tiled=True)  335 us
    psum x1, waiting for transfers between devices, body(): lax.psum(project_share.astype(jnp.bfloat16), 'seq').astype(jnp.float32)  297 us
    dot_general x38, matrix products, contract(): return jnp.einsum(form, left, right, preferred_element_type=jnp.float32)  225 us
    ppermute x3, waiting for transfers between devices, grow_blocks(): other = lax.ppermute(blocks, axis, [(i, i ^ bit) for i in range(size)])  180 us
    unnamed x218, local copies, waits for them, and re-layouts  147 us
    reduce_scatter x1, waiting for transfers between devices, body(): lax.psum_scatter(grad_up.astype(jnp.bfloat16), 'shard', scatter_dimension...  130 us
    reduce_scatter x1, waiting for transfers between devices, body(): lax.psum_scatter(grad_down.astype(jnp.bfloat16), 'shard', scatter_dimensi...  130 us
    unnamed x19, waiting for transfers between devices  95.2 us
  transfers between devices with their start and end apart: 21, of which 13 were waited for; matrix products, arithmetic and copies ran while one was open for 20% of the time, Pallas kernels for 0%

profile of v1, /device:TPU:0, one launch (start us, length us, event | category | flops | bytes accessed | tf_op | source)
XLA Modules:
  0.0 2066.7 jit_solution(1067788886525780577)
XLA Ops:
  25.8 175.3 %collective-permute-done.1 = bf16[2,768,1536]{2,1,0:T(8,128)(2,1)} collective-permute-done((bf16[2,768,1536]{2,1,0:T(8,128)(2,1)}, bf16[2,768,1536]{2,1,0:T(8,128)(2,1)}, u32[]{:S(2)}, u32[]{:S(2)}) %collective-permute-start.1) | collective-permute-done | bytes 4718624 | tf_op jit(solution)/shard_map/ppermute | solution.py:23
  210.3 13.1 reverse_select_fusion.1
  225.4 335.2 %all-gather = bf16[8,192,3]{1,2,0:T(4,128)(2,1)S(1)} all-gather(bf16[1,192,3]{1,2,0:T(4,128)(2,1)S(1)} %bitcast.389), channel_id=1, replica_groups=mesh['seq'=4,'shard'=8] {'shard'}, dimensions={0}, use_global_device_ids=true | all-gather | bytes 10368 | tf_op jit(solution)/shard_map/all_gather | solution.py:125
  589.5 16.8 pad_maximum_fusion
  606.2 52.8 %all-to-all-done = bf16[3,1,256,1536]{2,0,1,3:T(4,128)(2,1)} async-done(((bf16[3,1,256,1536]{2,0,1,3:T(4,128)(2,1)}), bf16[3,1,256,1536]{2,0,1,3:T(4,128)(2,1)}, u32[]{:S(2)}, u32[]{:S(2)}) %all-to-all-start) | async-done | bytes 2359328 | tf_op jit(solution)/shard_map/all_to_all | solution.py:167
  698.1 23.0 %reverse_select_fusion = bf16[2,4,768,1536]{3,2,1,0:T(8,128)(2,1)} fusion(bf16[2,4,768,1536]{3,2,1,0:T(8,128)(2,1)} %pad_maximum_fusion, pred[]{:T(512)S(6)} %eq.12), kind=kLoop, calls=%fused_computation.1 | loop fusion | flops 9437184 | bytes 37748736 | tf_op jit(solution)/shard_map/jit(_where)/select_n | solution.py:26
  749.3 24.1 %multiply_convert_fusion.2 = (bf16[256,6144]{1,0:T(8,128)(2,1)}, f32[256,6144]{1,0:T(8,128)}, f32[256,6144]{1,0:T(8,128)}) fusion(bf16[1536,6144]{1,0:T(8,128)(2,1)} %all-gather.16.cloned.1.call-done, f32[1,256,1536]{2,1,0:T(8,128)S(1)} %get-tuple-element.194, f32[1536]{0:T(1024)S(1)} %get-tuple-element.161, f32[1536]{0:T(1024)S(1)} %get-tuple-element.208, ...), kind=kOutput, calls=%fused_computation.37 | convolution fusion | flops 4936040448 | bytes 36190208 | tf_op jit(solution)/shard_map/cfd,dk->cfk/dot_general | solution.py:45
  773.4 21.4 %add_convert_fusion = bf16[256,6144]{1,0:T(8,128)(2,1)S(1)} fusion(f32[256,6144]{1,0:T(8,128)} %get-tuple-element.177, bf16[6144,1536]{1,0:T(8,128)(2,1)} %bitcast.348, f32[256,6144]{1,0:T(8,128)} %get-tuple-element.195, bf16[1,256,1536]{2,1,0:T(8,128)(2,1)S(1)} %copy-done.19), kind=kOutput, calls=%fused_computation.36 | convolution fusion | flops 4853858304 | bytes 35389440 | tf_op jit(solution)/shard_map/cfd,kd->cfk/dot_general | solution.py:45
  839.7 24.7 %all-reduce.7.cloned.1.call-done = bf16[2,64,1536]{2,1,0:T(8,128)(2,1)} async-done(((bf16[2,64,1536]{2,1,0:T(8,128)(2,1)}), bf16[2,64,1536]{2,1,0:T(8,128)(2,1)}) %all-reduce.7.cloned.1.call-update) | async-done | bytes 393232 | tf_op jit(solution)/shard_map/psum | solution.py:234
  874.5 30.8 %copy.233 = bf16[3,1536,1536]{2,0,1:T(4,128)(2,1)} copy(bf16[3,1536,1536]{1,2,0:T(8,128)(2,1)} %pad_maximum_fusion.1) | data formatting | bytes 28311552
  905.3 17.0 copy.241
  947.3 18.2 all-to-all-done.2
  1036.8 72.8 %all_to_all.60 = bf16[3,1,1024,384]{3,0,1,2:T(4,128)(2,1)S(1)} all-to-all(bf16[3,1,1024,384]{3,0,1,2:T(4,128)(2,1)S(1)} %pad_maximum_fusion.4), channel_id=1, replica_groups=mesh['seq'=4,'shard'=8] {'seq'}, dimensions={2} | all-to-all | bytes 4718592 | tf_op jit(solution)/shard_map/all_to_all | solution.py:263
  1124.8 30.8 %copy.231 = bf16[3,1536,1536]{2,0,1:T(4,128)(2,1)} copy(bf16[3,1536,1536]{1,2,0:T(8,128)(2,1)} %convert_bitcast_fusion) | data formatting | bytes 28311552
  1155.6 17.1 copy.240
  1185.0 12.9 convolution_convert_fusion.1
  1233.6 40.3 %reduce-scatter.29.cloned.1.call-done = bf16[192,4608]{1,0:T(8,128)(2,1)} async-done(((bf16[1536,4608]{1,0:T(8,128)(2,1)}), bf16[192,4608]{1,0:T(8,128)(2,1)}) %reduce-scatter.29.cloned.1.call-update) | async-done | bytes 1769488
  1284.6 47.1 %reduce-scatter.19.cloned.1.call-done = bf16[192,1536]{1,0:T(8,128)(2,1)} async-done(((bf16[1536,1536]{1,0:T(8,128)(2,1)}), bf16[192,1536]{1,0:T(8,128)(2,1)}) %reduce-scatter.19.cloned.1.call-update) | async-done | bytes 589840 | tf_op jit(solution)/shard_map/reduce_scatter | solution.py:246
  1331.7 57.7 %reduce-scatter.17.cloned.1.call-done = bf16[192,1536]{1,0:T(8,128)(2,1)} async-done(((bf16[1536,1536]{1,0:T(8,128)(2,1)}), bf16[192,1536]{1,0:T(8,128)(2,1)}) %reduce-scatter.17.cloned.1.call-update) | async-done | bytes 589840 | tf_op jit(solution)/shard_map/reduce_scatter | solution.py:274
  1389.4 130.1 %reduce-scatter.21.cloned.1.call-done = bf16[192,6144]{1,0:T(8,128)(2,1)} async-done(((bf16[1536,6144]{1,0:T(8,128)(2,1)}), bf16[192,6144]{1,0:T(8,128)(2,1)}) %reduce-scatter.21.cloned.1.call-update) | async-done | bytes 2359312 | tf_op jit(solution)/shard_map/reduce_scatter | solution.py:211
  1519.5 129.9 %reduce-scatter.23.cloned.1.call-done = bf16[768,1536]{1,0:T(8,128)(2,1)} async-done(((bf16[6144,1536]{1,0:T(8,128)(2,1)}), bf16[768,1536]{1,0:T(8,128)(2,1)}) %reduce-scatter.23.cloned.1.call-update) | async-done | bytes 2359312 | tf_op jit(solution)/shard_map/reduce_scatter | solution.py:214
  1670.8 15.6 reduce-scatter.25.cloned.1.call-done
  1687.3 36.0 %reduce-scatter.27.cloned.1.call-done = bf16[192,3]{1,0:T(8,128)(2,1)} async-done(((bf16[1536,3]{1,0:T(8,128)(2,1)}), bf16[192,3]{1,0:T(8,128)(2,1)}) %reduce-scatter.27.cloned.1.call-update) | async-done | bytes 1168
  1742.1 297.0 %all-reduce.9.cloned.1.call-done = (bf16[3,192,1536]{1,2,0:T(8,128)(2,1)}, bf16[192,1536]{1,0:T(8,128)(2,1)}, bf16[1,192,1536]{1,2,0:T(8,128)(2,1)}, bf16[192,15...) async-done(((bf16[3,192,1536]{1,2,0:T(8,128)(2,1)}, bf16[192,1536]{1,0:T(8,128)(2,1)}, bf16[1,192,1536]{1,2,0:T(8,128)(2,1)}, ...) | async-done | bytes 8257552 | tf_op jit(solution)/shard_map/psum | solution.py:285
  (393 shorter events, 411.4 us)
Async XLA Ops:
  7.2 713.9 %copy-start = (bf16[1,64,1536]{2,1,0:T(8,128)(2,1)S(1)}, bf16[1,64,1536]{2,1,0:T(8,128)(2,1)}, u32[]{:S(2)}) copy-start(bf16[1,64,1536]{2,1,0:T(8,128)(2,1)} %param.24) | copy-start | bytes 589828
  7.2 562.2 %all-gather.8.cloned.1.call-start = ((), (), s32[]{:S(2)}) async-start(), calls=%async_computation.12 | async-start | bytes 15925248 | tf_op jit(solution)/shard_map/all_gather | solution.py:123
  7.9 713.1 %all-gather.12.cloned.1.call-start = ((), (), s32[]{:S(2)}) async-start(), calls=%async_computation.14 | async-start | bytes 15925248 | tf_op jit(solution)/shard_map/all_gather | solution.py:132
  8.7 720.9 %all-gather.10.cloned.1.call-start = ((), (), s32[]{:S(2)}) async-start(), calls=%async_computation.13 | async-start | bytes 5308416 | tf_op jit(solution)/shard_map/all_gather | solution.py:124
  9.4 735.5 %all-gather.14.cloned.1.call-start = ((), (), s32[]{:S(2)}) async-start(), calls=%async_computation.15 | async-start | bytes 5308416 | tf_op jit(solution)/shard_map/all_gather | solution.py:133
  10.0 739.3 %all-gather.16.cloned.1.call-start = ((), (), s32[]{:S(2)}) async-start(), calls=%async_computation.16 | async-start | bytes 21233664 | tf_op jit(solution)/shard_map/all_gather | solution.py:139
  10.6 4.9 collective-permute-start
  23.1 177.9 %collective-permute-start.1 = (bf16[2,768,1536]{2,1,0:T(8,128)(2,1)}, bf16[2,768,1536]{2,1,0:T(8,128)(2,1)}, u32[]{:S(2)}, u32[]{:S(2)}) collective-permute-start(bf16[2,768,1536]{2,1,0:T(8,128)(2,1)} %get-tuple-element.179), channel_id=1, source_target_pairs={{0,2},{1,3},{2,0},{3,1},{4,6},{5,7},{6,4},{7,5},{8,10},{9,11},{10,... | collective-permute-start | bytes 14155784 | tf_op jit(solution)/shard_map/ppermute | solution.py:23
  210.3 350.3 %copy-start.92 = (bf16[3,192]{1,0:T(4,128)(2,1)S(1)}, bf16[3,192]{1,0:T(4,128)(2,1)}, u32[]{:S(2)}) copy-start(bf16[3,192]{1,0:T(4,128)(2,1)} %param.26) | copy-start | bytes 3460
  210.3 358.4 %copy-start.5 = (bf16[1,256,1536]{2,1,0:T(8,128)(2,1)S(1)}, bf16[1,256,1536]{2,1,0:T(8,128)(2,1)}, u32[]{:S(2)}) copy-start(bf16[1,256,1536]{2,1,0:T(8,128)(2,1)} %param.23) | copy-start | bytes 2359300
  223.4 366.0 %collective-permute-start.2 = (bf16[4,768,1536]{2,1,0:T(8,128)(2,1)}, bf16[4,768,1536]{2,1,0:T(8,128)(2,1)}, u32[]{:S(2)}, u32[]{:S(2)}) collective-permute-start(bf16[4,768,1536]{2,1,0:T(8,128)(2,1)} %bitcast.346), channel_id=1, source_target_pairs={{0,4},{1,5},{2,6},{3,7},{4,0},{5,1},{6,2},{7,3},{8,12},{9,13},{10,... | collective-permute-start | bytes 28311560 | tf_op jit(solution)/shard_map/ppermute | solution.py:23
  582.4 76.6 %all-to-all-start = ((bf16[3,1,256,1536]{2,0,1,3:T(4,128)(2,1)}), bf16[3,1,256,1536]{2,0,1,3:T(4,128)(2,1)}, u32[]{:S(2)}, u32[]{:S(2)}) async-start(bf16[3,1,256,1536]{2,0,1,3:T(4,128)(2,1)} %copy.193), calls=%async_computation | async-start | bytes 6291456 | tf_op jit(solution)/shard_map/all_to_all | solution.py:167
  694.5 33.9 %all-to-all-start.1 = ((bf16[4,2,49152]{2,1,0:T(2,128)(2,1)}), bf16[4,2,49152]{2,1,0:T(2,128)(2,1)S(1)}, u32[]{:S(2)}, u32[]{:S(2)}) async-start(bf16[4,2,49152]{2,1,0:T(2,128)(2,1)} %reshape.964), calls=%async_computation.1 | async-start | bytes 1572864 | tf_op jit(solution)/shard_map/all_to_all | solution.py:172
  698.0 166.4 %all-reduce.7.cloned.1.call-start = ((), (), s32[]{:S(2)}) async-start(), calls=%async_computation.17 | async-start | bytes 786432 | tf_op jit(solution)/shard_map/psum | solution.py:234
  826.9 397.4 %reduce-scatter.31.cloned.1.call-start = ((), (), s32[]{:S(2)}) async-start(), calls=%async_computation.25 | async-start | bytes 15925248
  943.5 22.0 %all-to-all-start.2 = ((bf16[4,2,49152]{2,1,0:T(2,128)(2,1)}), bf16[4,2,49152]{2,1,0:T(2,128)(2,1)S(1)}, u32[]{:S(2)}, u32[]{:S(2)}) async-start(bf16[4,2,49152]{2,1,0:T(2,128)(2,1)} %reshape.966), calls=%async_computation.2 | async-start | bytes 1572864 | tf_op jit(solution)/shard_map/all_to_all | solution.py:256
  947.3 326.6 %reduce-scatter.29.cloned.1.call-start = ((), (), s32[]{:S(2)}) async-start(), calls=%async_computation.24 | async-start | bytes 15925248
  1172.7 159.0 %reduce-scatter.19.cloned.1.call-start = ((), (), s32[]{:S(2)}) async-start(), calls=%async_computation.19 | async-start | bytes 5308416 | tf_op jit(solution)/shard_map/reduce_scatter | solution.py:246
  1178.0 211.3 %reduce-scatter.17.cloned.1.call-start = ((), (), s32[]{:S(2)}) async-start(), calls=%async_computation.18 | async-start | bytes 5308416 | tf_op jit(solution)/shard_map/reduce_scatter | solution.py:274
  1184.3 335.2 %reduce-scatter.21.cloned.1.call-start = ((), (), s32[]{:S(2)}) async-start(), calls=%async_computation.20 | async-start | bytes 21233664 | tf_op jit(solution)/shard_map/reduce_scatter | solution.py:211
  1197.9 451.6 %reduce-scatter.23.cloned.1.call-start = ((), (), s32[]{:S(2)}) async-start(), calls=%async_computation.21 | async-start | bytes 21233664 | tf_op jit(solution)/shard_map/reduce_scatter | solution.py:214
  1209.3 477.1 %reduce-scatter.25.cloned.1.call-start = ((), (), s32[]{:S(2)}) async-start(), calls=%async_computation.22 | async-start | bytes 442368
  1222.9 500.4 %reduce-scatter.27.cloned.1.call-start = ((), (), s32[]{:S(2)}) async-start(), calls=%async_computation.23 | async-start | bytes 442368
  1224.0 815.1 %all-reduce.9.cloned.1.call-start = ((), (), s32[]{:S(2)}) async-start(), calls=%async_computation.26 | async-start | bytes 18087936 | tf_op jit(solution)/shard_map/psum | solution.py:285
  (95 other events, 1264.4 us)
Sparse Core Ops, SparseCore 0:
  9.9 133.7 all-gather.7
  145.6 111.1 all-gather.11
  258.7 57.8 all-gather.9
  318.4 57.9 all-gather.13
  378.1 174.6 all-gather.15
  827.0 37.3 all-reduce.6
  922.6 101.5 reduce-scatter.30
  1172.8 101.0 reduce-scatter.28
  1277.9 53.7 reduce-scatter.18
  1335.6 53.7 reduce-scatter.16
  1393.0 126.4 reduce-scatter.20
  1523.0 126.4 reduce-scatter.22
  1652.5 33.9 reduce-scatter.24
  1689.4 33.8 reduce-scatter.26
  1727.0 312.0 all-reduce.8
